TPU v7x, 32 devices: a whole 2x2x4 slice. The times are simulated.
32 devices in a mesh: dp: 8 (over z, x), tensor: 4 (over y, core).
Axes of the slice: x: 2, y: 2, z: 4, core: 2. Of those that a mesh axis runs over, the one named last changes fastest.
Arguments:
- block_in: bfloat16 [2048, 8, 1024], P('tensor', 'dp'), may hold values from -6 to 6
- lengths: int32 [8, 8], P('dp'), may hold values from 1 to 2041, as said below
- qkv_weight: bfloat16 [1024, 3, 1024], P(None, None, 'tensor'), may hold values from -0.1875 to 0.1875
- out_weight: bfloat16 [1024, 1024], P('tensor'), may hold values from -0.1875 to 0.1875
- up_weight: bfloat16 [1024, 4096], P(None, 'tensor'), may hold values from -0.1875 to 0.1875
- down_weight: bfloat16 [4096, 1024], P('tensor'), may hold values from -0.09375 to 0.09375
- norm_gain: float32 [4, 1024], replicated, may hold values from 0.25 to 1.75
- norm_bias: float32 [4, 1024], replicated, may hold values from -2 to 2
- cotangent: bfloat16 [2048, 8, 1024], P('tensor', 'dp'), may hold values from -6 to 6
Outputs:
- block_out: bfloat16 [2048, 8, 1024], P('tensor', 'dp')
- input_grad: float32 [2048, 8, 1024], P('tensor', 'dp')
- qkv_grad: float32 [1024, 3, 1024], P(None, None, 'tensor')
- out_grad: float32 [1024, 1024], P('tensor')
- up_grad: float32 [1024, 4096], P(None, 'tensor')
- down_grad: float32 [4096, 1024], P('tensor')
- gain_grad: float32 [4, 1024], replicated
- bias_grad: float32 [4, 1024], replicated
Inputs may be any that keep to these rules, and one draw needn't show every extreme that they name: The 8 lengths of a row sum to 2048; one document of each row is longer than all others of the row together.
All inputs are finite; a program needn't handle non-finite values.
Results may differ from a plain program's by a relative error of at most 0.015.
Values may be sent and summed in bfloat16 or wider, within the bound.
A program may use at most 192 MiB of HBM per device.

v0:
```python
import functools

import jax
import jax.numpy as jnp
import numpy as np
from jax import lax
from jax.experimental import pallas as pl
from jax.experimental.pallas import tpu as pltpu
from jax.sharding import PartitionSpec as P

HD = 64
PAIR = 128
EPSILON = 1e-05
ROPE_BASE = 10000.0
NEG = -1e30
MESH = pl.DeviceIdType.MESH
BF = jnp.bfloat16
F32 = jnp.float32
NT = (((1,), (1,)), ((), ()))
NN = (((1,), (0,)), ((), ()))
TN = (((0,), (0,)), ((), ()))


def dot(a, b, dims=NN):
    return lax.dot_general(a, b, dims, preferred_element_type=F32)


def layer_norm(values, gain, shift):
    centre = values - jnp.mean(values, axis=-1, keepdims=True)
    spread = jnp.mean(centre * centre, axis=-1, keepdims=True)
    return centre * lax.rsqrt(spread + EPSILON) * gain + shift


def flip(index, offset):
    bit = 1
    while bit <= offset:
        if offset & bit:
            index = index + bit - 2 * bit * lax.rem(lax.div(index, bit), 2)
        bit *= 2
    return index


def xor(a, b, size):
    total, bit = 0, 1
    while bit < size:
        total = total + bit * lax.rem(lax.div(a, bit) + lax.div(b, bit), 2)
        bit *= 2
    return total


def greet(axes):
    barrier = pltpu.get_barrier_semaphore()
    count = 0
    for axis in axes:
        index = lax.axis_index(axis)
        for d in range(1, lax.axis_size(axis)):
            pl.semaphore_signal(barrier, inc=1, device_id={axis: flip(index, d)}, device_id_type=MESH)
            count += 1
    pl.semaphore_wait(barrier, count)


def tree_sum(parts):
    parts = [part.astype(F32) for part in parts]
    while len(parts) > 1:
        parts = [parts[i] + parts[i + 1] for i in range(0, len(parts), 2)]
    return parts[0]


def push(src, dst, sems, slot, axis, offset):
    return pltpu.make_async_remote_copy(
        src_ref=src,
        dst_ref=dst,
        send_sem=sems.at[0, slot],
        recv_sem=sems.at[1, slot],
        device_id={axis: flip(lax.axis_index(axis), offset)},
        device_id_type=MESH,
    )


def turn(values, cosine, signed_sine):
    lane = lax.broadcasted_iota(jnp.int32, values.shape, 1)
    other = jnp.where(lane % HD < HD // 2, pltpu.roll(values, PAIR - HD // 2, 1), pltpu.roll(values, HD // 2, 1))
    return values * cosine + other * signed_sine


def head_mask(shape, head):
    lane = lax.broadcasted_iota(jnp.int32, shape, 1)
    return lane // HD == head


def document_start(lengths_ref, spot):
    begin = jnp.zeros_like(spot)
    total = jnp.int32(0)
    for j in range(lengths_ref.shape[1] - 1):
        total = total + lengths_ref[0, j]
        begin = jnp.where(spot >= total, total, begin)
    return begin


def forward_kernel(block, ranks, pairs, chunks, *refs):
    lengths_ref, x_ref, gain_ref, shift_ref, w_ref, freq_ref, *refs = refs
    weights, refs = refs[:3], refs[3:]
    mixed_ref, log_ref, heads_ref, qkv_out, attn_out, cos_out, sin_out, *refs = refs
    rests, refs = refs[:3], refs[3:]
    scores_ref, qkv_ref, attn_ref, cos_ref, sin_ref, start_ref, out_sems, attn_sems, head_sems, own_sems, y_sems, z_sems, x_sems, core_sems = refs

    mine = lax.axis_index("tensor")
    rank = lax.axis_index("dp")
    group = lax.axis_size("dp") // 2
    x_bit, z_place = lax.rem(rank, 2), lax.div(rank, 2)
    direct = len(chunks) - 1
    started = []

    def start(copy):
        copy.start()
        started.append(copy)
        return copy

    outward = [
        pltpu.make_async_copy(src, dst, out_sems.at[i])
        for i, (src, dst) in enumerate(
            [(attn_ref, attn_out), (qkv_ref, qkv_out), (cos_ref, cos_out), (sin_ref, sin_out)]
        )
    ]

    def cut(array, c, *lead):
        at, (_, low, size) = array.at, chunks[c]
        return at[(*lead, slice(None), pl.ds(low, size))]

    def every(array, c, *lead):
        at, (_, low, size) = array.at, chunks[c]
        return at[(*lead, slice(None), slice(None), pl.ds(low, size))]

    def rest(c):
        return rests[chunks[c][0]]

    y_copies = [
        push(
            cut(weights[chunks[c][0]], c, x_bit, z_place), cut(rest(c), c, 1, x_bit, z_place), y_sems, c, "tensor", 2
        )
        for c in range(direct)
    ]
    whole = lambda array, c, *lead: array.at[(*lead, slice(None), slice(None), slice(None), pl.ds(*chunks[c][1:]))]
    y_copies.append(
        push(whole(weights[chunks[direct][0]], direct), whole(rest(direct), direct, 1), y_sems, direct, "tensor", 2)
    )
    z_copies = [
        [
            push(
                cut(rest(c), c, 1, x_bit, z_place),
                cut(rest(c), c, 1, x_bit, z_place),
                z_sems,
                c * (group - 1) + d - 1,
                "dp",
                2 * d,
            )
            for d in range(1, group)
        ]
        for c in range(direct)
    ]
    x_copies = [
        push(every(rest(c), c, 1, x_bit), every(rest(c), c, 1, x_bit), x_sems, c, "dp", 1) for c in range(direct - 1)
    ]
    core_copies = {
        c: push(whole(rest(c), c, 1), whole(rest(c), c, 2), core_sems, c, "tensor", 1)
        for c in [*range(direct - 1), direct]
    }
    own_copies = [push(weights[a], rests[a].at[0], own_sems, a, "tensor", 1) for a in range(3)]

    def to_z(c):
        y_copies[c].wait_recv()
        for copy in z_copies[c]:
            copy.start()

    def to_x(c):
        for copy in z_copies[c]:
            copy.wait_recv()
        x_copies[c].start()

    def to_core(c):
        (y_copies if c == direct else x_copies)[c].wait_recv()
        core_copies[c].start()

    greet(("tensor", "dp"))
    for c in range(direct - 1):
        y_copies[c].start()

    strips = 4
    strip = block // strips
    gain, shift = gain_ref[0:1, :], shift_ref[0:1, :]
    across, beside, onward = [], [], []
    for q in range(strips):

        @pl.loop(0, strip // 64)
        def _(r):
            at = pl.ds(pl.multiple_of(q * strip + r * 64, 64), 64)
            attn_ref[0, at, :] = layer_norm(x_ref[at, :].astype(F32), gain, shift).astype(BF)

        at = pl.ds(q * strip, strip)
        across.append(start(push(attn_ref.at[0, at], attn_ref.at[2, at], attn_sems, q, "tensor", 2)))
        beside.append(start(push(attn_ref.at[0, at], attn_ref.at[1, at], attn_sems, strips + q, "tensor", 1)))
        onward.append(push(attn_ref.at[2, at], attn_ref.at[3, at], attn_sems, 2 * strips + q, "tensor", 1))

    y_copies[direct - 1].start()
    to_z(0)

    lane = lax.broadcasted_iota(jnp.int32, (64, PAIR), 1)
    sign = jnp.where(lane % HD < HD // 2, -1.0, 1.0)

    @pl.loop(0, ranks * block // 64)
    def _(r):
        at = pl.ds(pl.multiple_of(r * 64, 64), 64)
        spot = r * 64 + lax.broadcasted_iota(jnp.int32, (64, PAIR), 0)
        begin = document_start(lengths_ref, spot)
        start_ref[at, :] = begin
        angle = (spot - begin).astype(F32) * freq_ref[...]
        cos_ref[at, :] = jnp.cos(angle)
        sin_ref[at, :] = jnp.sin(angle) * sign

    def middle():
        to_x(0)
        to_z(1)
        for q in range(strips - 1):
            across[q].wait_recv()
            onward[q].start()
        to_x(1)
        to_z(2)
        across[strips - 1].wait_recv()
        onward[strips - 1].start()
        y_copies[direct].start()
        for copy in own_copies:
            copy.start()

    def beside_here():
        for copy in beside:
            copy.wait_recv()

    def onward_here():
        for copy in onward:
            copy.wait_recv()

    @pl.loop(0, ranks)
    def _(d):
        pl.when(d == 1)(beside_here)
        pl.when(d == 2)(middle)
        pl.when(d == 3)(onward_here)
        x = attn_ref[d]
        rows = pl.ds(pl.multiple_of(d * block, block), block)
        real = pl.ds(pl.multiple_of(xor(d, mine, ranks) * block, block), block)
        for part in range(3):
            project = dot(x, w_ref[part])
            for pair in range(pairs):
                piece = project[:, pair * PAIR : (pair + 1) * PAIR]
                if part < 2:
                    piece = turn(piece, cos_ref[real, :], sin_ref[real, :])
                qkv_ref[part * pairs + pair, rows, :] = piece.astype(BF)

    sub = block // 2

    def unit(pair, d):
        row_block = xor(d, mine, ranks)
        rows = pl.ds(pl.multiple_of(d * block, block), block)
        begin = start_ref[pl.ds(pl.multiple_of(row_block * block, block), block), :]
        queries = qkv_ref[pair, rows, :] * HD**-0.5
        heads = range(PAIR // HD)
        masks = [head_mask(queries.shape, head) for head in heads]
        parts = [jnp.where(mask, queries, jnp.zeros_like(queries)) for mask in masks]
        column = lax.broadcasted_iota(jnp.int32, (block, 128), 1)

        def score(j, tops, last):
            at = pl.ds(pl.multiple_of(xor(j, mine, ranks) * block, block), block)
            keys = qkv_ref[pairs + pair, at, :]
            tops = list(tops)
            for low in range(0, block, sub):
                for head in heads:
                    s = dot(parts[head], keys[low : low + sub], NT)
                    for c in range(0, sub, 128):
                        visible = column + (low + c) >= begin - j * block
                        if last:
                            visible &= column + (low + c) <= lax.broadcasted_iota(jnp.int32, (block, 128), 0)
                        piece = jnp.where(visible, s[:, c : c + 128], NEG)
                        scores_ref[head, j, :, low + c : low + c + 128] = piece
                        tops[head] = jnp.maximum(tops[head], piece)
            return tuple(tops)

        tops = tuple(jnp.full((block, 128), NEG, F32) for _ in heads)
        tops = lax.fori_loop(0, row_block, lambda j, tops: score(j, tops, False), tops)
        tops = score(row_block, tops, True)
        tops = [jnp.broadcast_to(jnp.max(top, axis=1, keepdims=True), (block, 128)) for top in tops]

        def mix(j, accs):
            at = pl.ds(pl.multiple_of(xor(j, mine, ranks) * block, block), block)
            values = qkv_ref[2 * pairs + pair, at, :]
            accs = list(accs)
            for low in range(0, block, sub):
                for head in heads:
                    filled = jnp.where(masks[head], values, jnp.ones_like(values))[low : low + sub]
                    shares = [
                        jnp.exp(scores_ref[head, j, :, low + c : low + c + 128] - tops[head]).astype(BF)
                        for c in range(0, sub, 128)
                    ]
                    accs[head] = accs[head] + dot(jnp.concatenate(shares, axis=1), filled)
            return tuple(accs)

        accs = lax.fori_loop(0, row_block + 1, mix, tuple(jnp.zeros((block, PAIR), F32) for _ in heads))
        totals = [pltpu.roll(acc, HD, 1) for acc in accs]
        mixed_ref[pair, rows, :] = jnp.where(masks[0], accs[0] / totals[0], accs[1] / totals[1]).astype(BF)
        for head in heads:
            logs = tops[head] + jnp.log(jnp.where(masks[head], totals[head], accs[head]))
            log_ref[pair, head : head + 1, rows] = jnp.transpose(logs)[0:1, :]

    def head_copy(pair, d):
        slot = d * pairs + pair
        return pltpu.make_async_remote_copy(
            src_ref=mixed_ref.at[pair, pl.ds(pl.multiple_of(d * block, block), block)],
            dst_ref=heads_ref.at[slot],
            send_sem=head_sems.at[0, slot],
            recv_sem=head_sems.at[1, slot],
            device_id={"tensor": xor(mine, d, ranks)},
            device_id_type=MESH,
        )

    for copy in outward:
        copy.start()
    units = pairs * ranks
    events = {
        0: [lambda: to_x(2), lambda: to_z(3), lambda: to_z(4), lambda: to_core(0), lambda: to_core(1)],
        3: [lambda: to_x(3)],
        5: [lambda: to_core(2)],
    }

    @pl.loop(0, units)
    def _(u):
        pair, d = lax.rem(u, pairs), ranks - 1 - lax.div(u, pairs)
        unit(pair, d)
        pl.when(d > 0)(lambda: head_copy(pair, d).start())
        for when, steps in events.items():

            @pl.when(u == min(when, units - 1))
            def _():
                for step in steps:
                    step()

    for pair in range(pairs):
        heads_ref[pair] = mixed_ref[pair, 0:block, :]
    to_core(3)
    to_core(direct)

    @pl.loop(pairs, units)
    def _(slot):
        copy = head_copy(lax.rem(slot, pairs), lax.div(slot, pairs))
        copy.wait_recv()
        copy.wait_send()

    for copy in [*core_copies.values(), *own_copies, *z_copies[direct - 1]]:
        copy.wait_recv()
    for copy in [*started, *onward, *own_copies, *y_copies, *x_copies, *core_copies.values()]:
        copy.wait_send()
    for copies in z_copies:
        for copy in copies:
            copy.wait_send()
    for copy in outward:
        copy.wait()


def attend_forward(lengths, tokens, gains, shifts, weight, weights):
    block, width = tokens.shape
    ranks = lax.axis_size("tensor")
    assert ranks == 4
    length = block * ranks
    pairs = weight.shape[2] // PAIR
    group = lax.axis_size("dp") // 2
    views = [w.reshape(2, group, w.shape[0] // (2 * group), w.shape[1]) for w in weights]
    chunks = [(0, 0, width)]
    for a in (1, 2):
        columns = weights[a].shape[1] // 2
        chunks += [(a, 0, columns), (a, columns, columns)]
    chunks[3:] = [(2, columns, columns // 2), (2, 0, columns), (2, columns + columns // 2, columns // 2)]
    vmem = pl.BlockSpec(memory_space=pltpu.VMEM)
    hbm = pl.BlockSpec(memory_space=pl.ANY)
    copies = pltpu.SemaphoreType.DMA
    lane = np.arange(PAIR) % (HD // 2)
    frequencies = jnp.asarray((ROPE_BASE ** (-lane * 2.0 / HD))[None, :], F32)
    smem = pl.BlockSpec(memory_space=pltpu.SMEM)
    mixed, logs, heads, qkv, attn, cosine, sine, *rests = pl.pallas_call(
        functools.partial(forward_kernel, block, ranks, pairs, chunks),
        out_shape=[
            jax.ShapeDtypeStruct((pairs, length, PAIR), BF),
            jax.ShapeDtypeStruct((pairs, 8, length), F32),
            jax.ShapeDtypeStruct((ranks * pairs, block, PAIR), BF),
            jax.ShapeDtypeStruct((3 * pairs, length, PAIR), BF),
            jax.ShapeDtypeStruct((ranks, block, width), BF),
            jax.ShapeDtypeStruct((length, PAIR), F32),
            jax.ShapeDtypeStruct((length, PAIR), F32),
            *[jax.ShapeDtypeStruct((ranks - 1, *view.shape), BF) for view in views],
        ],
        in_specs=[smem] + [vmem] * 5 + [hbm] * 3,
        out_specs=[vmem] * 3 + [hbm] * 7,
        scratch_shapes=[
            pltpu.VMEM((PAIR // HD, ranks, block, block), F32),
            pltpu.VMEM((3 * pairs, length, PAIR), BF),
            pltpu.VMEM((ranks, block, width), BF),
            pltpu.VMEM((length, PAIR), F32),
            pltpu.VMEM((length, PAIR), F32),
            pltpu.VMEM((length, PAIR), jnp.int32),
            copies((4,)),
            copies((2, 12)),
            copies((2, ranks * pairs)),
            copies((2, 3)),
            copies((2, len(chunks))),
            copies((2, len(chunks) * (group - 1))),
            copies((2, len(chunks))),
            copies((2, len(chunks))),
        ],
        compiler_params=pltpu.CompilerParams(vmem_limit_bytes=56 << 20, collective_id=2, has_side_effects=True),
        name="attend_forward",
    )(lengths, tokens, gains, shifts, weight, frequencies, *views)
    rests = [r.reshape(ranks - 1, *w.shape) for r, w in zip(rests, weights)]
    return qkv, attn, mixed, logs, heads, cosine, sine, rests


def unit_scale(values):
    centre = values - jnp.mean(values, axis=-1, keepdims=True)
    scale = lax.rsqrt(jnp.mean(centre * centre, axis=-1, keepdims=True) + EPSILON)
    return centre * scale, scale


def norm_pull(grad, unit, scale, gain):
    inside = grad * gain
    first = jnp.mean(inside, axis=-1, keepdims=True)
    second = jnp.mean(inside * unit, axis=-1, keepdims=True)
    return scale * (inside - first - unit * second)


def gelu_both(x):
    bend = 0.7978845608028654
    square = x * x
    t = jnp.tanh(bend * (x + 0.044715 * (square * x)))
    side = 0.5 * (1.0 + t)
    return x * side, side + 0.5 * x * (1.0 - t * t) * (bend * (1.0 + 0.134145 * square))


def middle_kernel(block, ranks, pairs, *refs):
    (heads_ref, x_ref, dy_ref, gains_ref, shifts_ref, *refs) = refs
    sources, refs = refs[:6], refs[6:]
    (out_ref, rest_ref, do_ref, shared_ref, down_ref, up_ref, got_down, got_up, early_ref, *refs) = refs
    (out_all, up_all, down_all, work_ref, mlp_ref, gmp_ref, middle_ref, proj_ref, acc_ref, gap_ref, gh_ref, *refs) = refs
    (out_sems, up_sems, down_sems, part_sems, cross_sems, mlp_sems, gmp_sems, head_sems, sum_sems) = refs

    mine = lax.axis_index("tensor")
    width = x_ref.shape[1]
    strips, rows = 4, 64
    strip = block // strips
    columns = width // 2

    def loads(own, rest, array, sems):
        return [
            pltpu.make_async_copy(own if d == 0 else rest.at[d - 1], array.at[d], sems.at[d]) for d in range(ranks)
        ]

    out_loads = loads(sources[0], sources[1], out_all, out_sems)
    up_loads = loads(sources[2], sources[3], up_all, up_sems)
    down_loads = loads(sources[4], sources[5], down_all, down_sems)[:2]
    rank = lax.axis_index("dp")
    near = pl.ds(pl.multiple_of(lax.rem(rank, 2) * columns, columns), columns)
    left, inner = pl.ds(0, columns), pl.ds(columns, columns)
    far_down = sources[5]
    part_loads = [
        pltpu.make_async_copy(far_down.at[1, near, left], down_all.at[2, near, left], part_sems.at[0]),
        pltpu.make_async_copy(far_down.at[1, :, inner], down_all.at[2, :, inner], part_sems.at[1]),
        pltpu.make_async_copy(far_down.at[2, :, inner], down_all.at[3, :, inner], part_sems.at[2]),
    ]
    part_copies = [
        push(far_down.at[1, near, left], down_all.at[2, near, left], cross_sems, 0, "dp", 1),
        push(down_all.at[2, :, left], down_all.at[3, :, left], cross_sems, 1, "tensor", 1),
    ]
    for copy in out_loads:
        copy.start()
    for d in range(ranks):
        up_loads[d].start()
        if d < 2:
            down_loads[d].start()
    for load in part_loads:
        load.start()
    greet(("tensor", "dp"))
    part_copies[0].start()

    def senders(array, sems):
        found = []
        for q in range(strips):
            at = pl.ds(q * strip, strip)
            found.append(
                (
                    push(array.at[0, at], array.at[2, at], sems, q, "tensor", 2),
                    push(array.at[0, at], array.at[1, at], sems, strips + q, "tensor", 1),
                    push(array.at[2, at], array.at[3, at], sems, 2 * strips + q, "tensor", 1),
                )
            )
        return found

    mlp_copies = senders(mlp_ref, mlp_sems)
    gmp_copies = senders(gmp_ref, gmp_sems)

    def send_strip(copies, q):
        copies[q][0].start()
        copies[q][1].start()

    def forward_on(copies):
        for across, _, onward in copies:
            across.wait_recv()
            onward.start()

    for d in range(ranks):
        out_loads[d].wait()
    for c in (0, columns):
        at = pl.ds(c, columns)
        total = None
        for d in range(ranks):
            part = jnp.concatenate([heads_ref[d * pairs + p] for p in range(pairs)], axis=1)
            term = dot(part, out_all[d, :, at])
            total = term if total is None else total + term
        proj_ref[:, at] = total

    gain = [gains_ref[j : j + 1, :] for j in range(4)]
    shift = [shifts_ref[j : j + 1, :] for j in range(4)]

    for q in range(strips):

        @pl.loop(0, strip // rows)
        def _(r):
            at = pl.ds(pl.multiple_of(q * strip + r * rows, rows), rows)
            unit, _ = unit_scale(proj_ref[at, :])
            middle = x_ref[at, :].astype(F32) + (unit * gain[1] + shift[1])
            middle_ref[at, :] = middle
            unit, _ = unit_scale(middle)
            mlp_ref[0, at, :] = (unit * gain[2] + shift[2]).astype(BF)

        send_strip(mlp_copies, q)

    acc_ref[...] = jnp.zeros_like(acc_ref)

    @pl.loop(0, ranks)
    def _(d):
        pltpu.make_async_copy(up_all.at[d], up_all.at[d], up_sems.at[d]).wait()

        @pl.when(d < 2)
        def _():
            pltpu.make_async_copy(down_all.at[d], down_all.at[d], down_sems.at[d]).wait()

        @pl.when(d == 2)
        def _():
            for load in part_loads[:2]:
                load.wait()
            part_copies[0].wait_recv()
            part_copies[1].start()

        @pl.when(d == 3)
        def _():
            part_loads[2].wait()
            part_copies[1].wait_recv()

        for c in (0, columns):
            at = pl.ds(c, columns)
            hidden, slope = gelu_both(dot(mlp_ref[0], up_all[d, :, at]))
            work_ref[d, :, at] = slope
            acc_ref[...] += dot(hidden.astype(BF), down_all[d, at, :])

    zero = jnp.zeros((1, width), F32)
    gain_three, shift_three = zero, zero
    for q in range(strips):

        def last_norm(r, carry):
            gain_term, shift_term = carry
            at = pl.ds(pl.multiple_of(q * strip + r * rows, rows), rows)
            unit, scale = unit_scale(acc_ref[at, :])
            out_ref[at, :] = (middle_ref[at, :] + (unit * gain[3] + shift[3])).astype(BF)
            dy = dy_ref[at, :].astype(F32)
            gmp_ref[0, at, :] = norm_pull(dy, unit, scale, gain[3]).astype(BF)
            return (
                gain_term + jnp.sum(dy * unit, axis=0, keepdims=True),
                shift_term + jnp.sum(dy, axis=0, keepdims=True),
            )

        gain_three, shift_three = lax.fori_loop(0, strip // rows, last_norm, (gain_three, shift_three))
        send_strip(gmp_copies, q)

    acc_ref[...] = jnp.zeros_like(acc_ref)

    @pl.loop(0, ranks)
    def _(d):
        for c in (0, columns):
            at = pl.ds(c, columns)
            grad = dot(gmp_ref[0], down_all[d, at, :], NT)
            grad = (grad * work_ref[d, :, at]).astype(BF)
            acc_ref[...] += dot(grad, up_all[d, :, at], NT)

    forward_on(mlp_copies)

    def inner_norms(r, carry):
        gain_two, shift_two, gain_one, shift_one = carry
        at = pl.ds(pl.multiple_of(r * rows, rows), rows)
        grad = acc_ref[at, :]
        unit, scale = unit_scale(middle_ref[at, :])
        gain_two = gain_two + jnp.sum(grad * unit, axis=0, keepdims=True)
        shift_two = shift_two + jnp.sum(grad, axis=0, keepdims=True)
        grad = dy_ref[at, :].astype(F32) + norm_pull(grad, unit, scale, gain[2])
        rest_ref[at, :] = grad
        unit, scale = unit_scale(proj_ref[at, :])
        gain_one = gain_one + jnp.sum(grad * unit, axis=0, keepdims=True)
        shift_one = shift_one + jnp.sum(grad, axis=0, keepdims=True)
        gap_ref[at, :] = norm_pull(grad, unit, scale, gain[1]).astype(BF)
        return gain_two, shift_two, gain_one, shift_one

    gain_two, shift_two, gain_one, shift_one = lax.fori_loop(0, block // rows, inner_norms, (zero, zero, zero, zero))
    early_ref[...] = jnp.concatenate(
        [zero, gain_one, gain_two, gain_three, zero, shift_one, shift_two, shift_three], axis=0
    )

    head_copies = []
    for d in [*range(1, ranks), 0]:
        grad = dot(gap_ref[...], out_all[d], NT).astype(BF)
        for pair in range(pairs):
            piece = grad[:, pair * PAIR : (pair + 1) * PAIR]
            if d == 0:
                do_ref[pair, 0] = piece
            else:
                slot = d * pairs + pair
                gh_ref[slot] = piece
                head_copies.append(push(gh_ref.at[slot], do_ref.at[pair, d], head_sems, slot, "tensor", d))
    for d in range(ranks):
        part = jnp.concatenate([heads_ref[d * pairs + p] for p in range(pairs)], axis=1)
        shared_ref[d] = dot(part, gap_ref[...], TN).astype(BF)

    for copies in (mlp_copies, gmp_copies):
        for _, beside, _ in copies:
            beside.wait_recv()
    work_ref[...] = jnp.zeros_like(work_ref)

    def late():
        forward_on(gmp_copies)
        for copy in head_copies:
            copy.start()

    def latest():
        for copies in (mlp_copies, gmp_copies):
            for _, _, onward in copies:
                onward.wait_recv()

    sums = [
        push(ref.at[0, 1 - lax.rem(lax.div(rank, 1 << o), 2)], got, sum_sems, o, "dp", 1 << o)
        for o, (ref, got) in enumerate([(down_ref, got_down), (up_ref, got_up)])
    ]
    half = columns // 2

    @pl.loop(0, 2 * ranks)
    def _(step):
        part = lax.div(step + 1, 3)
        i = step + 1 - 3 * part
        first, last, up = lax.div(2 - part, 2), lax.div(part, 2), lax.div(i + 1, 2)
        centre = 1 - first - last
        h = centre * (1 - up) + last
        b = first * (i - 1) + centre * (i + up) + last * (i + 1)
        pl.when(step == 3)(late)
        pl.when(step == 4)(latest)
        at = pl.ds(pl.multiple_of(h * columns, columns), columns)
        tokens, grads = mlp_ref[b], gmp_ref[b]
        hidden, slope = gelu_both(dot(tokens, up_all[0, :, at]))
        grad = (dot(grads, down_all[0, at, :], NT) * slope).astype(BF)
        work_ref[2 * h] += dot(hidden.astype(BF), grads, TN)
        work_ref[2 * h + 1, :, 0:columns] += dot(tokens[:, 0:columns], grad, TN)
        work_ref[2 * h + 1, :, columns:] += dot(tokens[:, columns:], grad, TN)

        @pl.when(b == ranks - 1)
        def _():
            for side in range(2):
                down_ref[h, side] = work_ref[2 * h, side * half : (side + 1) * half, :].astype(BF)
                up_ref[h, side] = work_ref[2 * h + 1, :, side * columns : (side + 1) * columns].astype(BF)

        @pl.when(step == 4)
        def _():
            for copy in sums:
                copy.start()

    for copy in sums:
        copy.wait()
    for copy in head_copies:
        copy.wait_recv()
        copy.wait_send()
    for copy in part_copies:
        copy.wait_send()
    for copies in (mlp_copies, gmp_copies):
        for group in copies:
            for copy in group:
                copy.wait_send()


def middle_stage(heads, tokens, cotangent, gains, shifts, weights, rests):
    block, width = tokens.shape
    ranks = lax.axis_size("tensor")
    local = weights[0].shape[0]
    pairs = local // PAIR
    hidden = weights[2].shape[0]
    vmem = pl.BlockSpec(memory_space=pltpu.VMEM)
    hbm = pl.BlockSpec(memory_space=pl.ANY)
    copies = pltpu.SemaphoreType.DMA
    assert block * 2 == width and hidden == width
    operands = [array for pair in zip(weights, rests) for array in pair]
    return pl.pallas_call(
        functools.partial(middle_kernel, block, ranks, pairs),
        out_shape=[
            jax.ShapeDtypeStruct((block, width), BF),
            jax.ShapeDtypeStruct((block, width), F32),
            jax.ShapeDtypeStruct((pairs, ranks, block, PAIR), BF),
            jax.ShapeDtypeStruct((ranks, local, width), BF),
            jax.ShapeDtypeStruct((2, 2, block // 2, width), BF),
            jax.ShapeDtypeStruct((2, 2, block, width // 2), BF),
            jax.ShapeDtypeStruct((block // 2, width), BF),
            jax.ShapeDtypeStruct((block, width // 2), BF),
            jax.ShapeDtypeStruct((8, width), F32),
        ],
        in_specs=[vmem] * 5 + [hbm] * 6,
        out_specs=[vmem] * 9,
        scratch_shapes=[
            pltpu.VMEM((ranks, local, width), BF),
            pltpu.VMEM((ranks, width, hidden), BF),
            pltpu.VMEM((ranks, hidden, width), BF),
            pltpu.VMEM((ranks, block, width), F32),
            pltpu.VMEM((ranks, block, width), BF),
            pltpu.VMEM((ranks, block, width), BF),
            pltpu.VMEM((block, width), F32),
            pltpu.VMEM((block, width), F32),
            pltpu.VMEM((block, width), F32),
            pltpu.VMEM((block, width), BF),
            pltpu.VMEM((ranks * pairs, block, PAIR), BF),
            copies((ranks,)),
            copies((ranks,)),
            copies((2,)),
            copies((3,)),
            copies((2, 2)),
            copies((2, 12)),
            copies((2, 12)),
            copies((2, ranks * pairs)),
            copies((2, 2)),
        ],
        compiler_params=pltpu.CompilerParams(vmem_limit_bytes=62 << 20, collective_id=3, has_side_effects=True),
        name="middle_stage",
    )(heads, tokens, cotangent, gains, shifts, *operands)


def finish_kernel(block, blocks, pairs, orders, *refs):
    (lengths_ref, down_ref, up_ref, first_down, first_up, shared_ref, log_ref, gain_ref, early_ref, *refs) = refs
    far_refs, refs = refs[:9], refs[9:]
    (input_ref, sums_ref, down_out, up_out, own_out, qkv_out, *refs) = refs
    near_refs, refs = refs[:9], refs[9:]
    (qkv_ref, do_ref, o_ref, cos_ref, sin_ref, attn_ref, w_ref, x_ref, rest_ref) = near_refs
    (start_ref, dq_ref, inner_ref, grads_ref, own_ref, wide_ref, token_ref, core_sum, got_y, *refs) = refs
    (token_sum, token_y, norm_ref, got_t, sum_t, got_d, *refs) = refs
    chunks, steps = len(orders), len(orders[0])
    count = chunks * steps
    got, refs = refs[:count], refs[count:]
    (load_sems, rs_sems, ag_sems, core_sems, y_sems, token_core_sems, token_y_sems, t_sems, d_sems) = refs

    mine = lax.axis_index("tensor")
    rank = lax.axis_index("dp")
    ranks_dp = lax.axis_size("dp")
    heads = PAIR // HD
    started = []
    loads = [
        pltpu.make_async_copy(far, near, load_sems.at[i]) for i, (far, near) in enumerate(zip(far_refs, near_refs))
    ]
    for load in loads:
        load.start()

    def start(copy):
        copy.start()
        started.append(copy)
        return copy

    sources = [down_ref.at[0], up_ref.at[0], down_ref.at[1], up_ref.at[1], own_ref] + [wide_ref.at[p] for p in range(pairs)]
    results = [down_out.at[0], up_out.at[0], down_out.at[1], up_out.at[1], own_out] + [qkv_out.at[p] for p in range(pairs)]
    firsts = {0: first_down, 1: first_up}
    bits = [[lax.rem(lax.div(rank, 1 << o), 2) for o in order] for order in orders]
    rs_copies, ag_copies = {}, {}

    def held(c, k):
        return sources[c] if k == 0 else got[c * steps + k - 1]

    for c in range(chunks):
        for k in range(steps):
            far = 1 << orders[c][k]
            if k > 0 or c not in firsts:
                source = held(c, k).at[1 - bits[c][k]]
                rs_copies[c, k] = push(source, got[c * steps + k], rs_sems, c * steps + k, "dp", far)
            region = results[c].at[tuple(bits[c][: k + 1])]
            ag_copies[c, k] = push(region, region, ag_sems, c * steps + k, "dp", far)

    def begin(c):
        rs_copies[c, 0].start()

    def halve(c, k):
        at = c * steps + k
        if (c, k) in rs_copies:
            rs_copies[c, k].wait_recv()
            term = got[at][...]
        else:
            term = firsts[c][...]
        total = held(c, k)[bits[c][k]].astype(F32) + term.astype(F32)
        got[at][...] = total.astype(BF)
        if k + 1 < steps:
            rs_copies[c, k + 1].start()
        else:
            results[c][tuple(bits[c])] = total.astype(BF)
            ag_copies[c, k].start()

    def double(c, k):
        ag_copies[c, k].wait_recv()
        if k > 0:
            ag_copies[c, k - 1].start()

    core_copies = [
        push(shared_ref.at[d + 1], core_sum.at[d // 2], core_sems, d // 2, "tensor", 1) for d in range(0, blocks, 2)
    ]
    y_copies = [
        push(core_sum.at[h], got_y.at[h - 1], y_sems, h - 1, "tensor", 2 * h) for h in range(1, blocks // 2)
    ]

    def pair_up():
        for h in range(blocks // 2):
            core_copies[h].wait_recv()
            core_sum[h] = (shared_ref[2 * h].astype(F32) + core_sum[h].astype(F32)).astype(BF)
        for copy in y_copies:
            copy.start()

    def settle():
        total = core_sum[0].astype(F32)
        for h in range(1, blocks // 2):
            y_copies[h - 1].wait_recv()
            total = total + got_y[h - 1].astype(F32)
        own_ref[...] = total.astype(BF)

    def prepare(pair):
        dq_ref[...] = jnp.zeros_like(dq_ref)
        for b in range(blocks):
            rows = pl.ds(b * block, block)
            product = do_ref[pair, b].astype(F32) * o_ref[pair, rows, :].astype(F32)
            high = product.astype(BF)
            low = (product - high.astype(F32)).astype(BF)
            for head in range(heads):
                ones = head_mask((16, PAIR), head).astype(F32).astype(BF)
                inner = dot(ones, high, NT) + dot(ones, low, NT)
                inner_ref[head : head + 1, rows] = inner[0:1, :]

    def unit(pair, key_block):
        slot = xor(key_block, mine, blocks)
        here = pl.ds(pl.multiple_of(slot * block, block), block)
        keys = qkv_ref[pairs + pair, here, :]
        values = qkv_ref[2 * pairs + pair, here, :]
        dk = jnp.zeros((block, PAIR), F32)
        dv = jnp.zeros((block, PAIR), F32)
        for head in range(heads):
            mask = head_mask(keys.shape, head)
            key = jnp.where(mask, keys * HD**-0.5, jnp.zeros_like(keys))
            value = jnp.where(mask, values, jnp.zeros_like(values))

            def one(i, carry, first):
                dk, dv = carry
                place = xor(i, mine, blocks)
                rows = pl.ds(pl.multiple_of(place * block, block), block)
                real = pl.ds(pl.multiple_of(i * block, block), block)
                query = qkv_ref[pair, rows, :]
                grad = do_ref[pair, place]
                s = dot(key, query, NT)
                row = lax.broadcasted_iota(jnp.int32, s.shape, 0)
                visible = row >= start_ref[0:1, real] - key_block * block
                if first:
                    visible &= row <= lax.broadcasted_iota(jnp.int32, s.shape, 1)
                probs = jnp.where(visible, jnp.exp(s - log_ref[pair, head : head + 1, rows]), 0.0)
                grad_probs = dot(value, grad, NT)
                ds = (probs * (grad_probs - inner_ref[head : head + 1, rows])).astype(BF)
                zero = jnp.zeros_like(query)
                dv = dv + dot(probs.astype(BF), jnp.where(mask, grad, zero))
                dk = dk + dot(ds, jnp.where(mask, query, zero))
                dq_ref[rows, :] += dot(ds, key, TN)
                return dk, dv

            dk, dv = one(key_block, (dk, dv), True)
            dk, dv = lax.fori_loop(key_block + 1, blocks, lambda i, carry: one(i, carry, False), (dk, dv))
        real = pl.ds(pl.multiple_of(key_block * block, block), block)
        grads_ref[pairs + pair, here, :] = turn(dk * HD**-0.5, cos_ref[real, :], -sin_ref[real, :]).astype(BF)
        grads_ref[2 * pairs + pair, here, :] = dv.astype(BF)

    def close(pair):
        for b in range(blocks):
            rows = pl.ds(b * block, block)
            real = pl.ds(pl.multiple_of(flip(mine, b) * block, block), block)
            grads_ref[pair, rows, :] = turn(dq_ref[rows, :], cos_ref[real, :], -sin_ref[real, :]).astype(BF)
        total = None
        for b in range(blocks):
            rows = pl.ds(b * block, block)
            wide = jnp.concatenate([grads_ref[c * pairs + pair, rows, :] for c in range(3)], axis=1)
            term = dot(attn_ref[b], wide, TN)
            total = term if total is None else total + term
        wide_ref[pair] = total.astype(BF).reshape(wide_ref.shape[1:])

    greet(("tensor", "dp"))
    for copy in core_copies:
        copy.start()
    begin(3)
    begin(2)
    halve(0, 0)
    halve(1, 0)
    start_ref[...] = document_start(lengths_ref, lax.broadcasted_iota(jnp.int32, start_ref.shape, 1))
    for load in loads[:5]:
        load.wait()
    slots = pairs * blocks
    halving = lambda *steps: [functools.partial(halve, c, k) for c, k in steps]
    doubling = lambda *steps: [functools.partial(double, c, k) for c, k in steps]
    beginning = lambda c: [functools.partial(begin, c)]
    events = {
        0: [pair_up],
        2: [settle] + beginning(4) + halving((0, 1), (3, 0), (1, 1), (2, 0)),
        3: [lambda: [load.wait() for load in loads[5:]]],
        4: beginning(5) + halving((0, 2), (4, 0), (3, 1), (1, 2)),
        5: halving((2, 1)),
        6: halving((4, 1)) + doubling((0, 2)),
        7: halving((3, 2)) + doubling((1, 2)),
    }

    @pl.loop(0, slots)
    def _(u):
        pair, key_block = lax.div(u, blocks), lax.rem(u, blocks)
        for when, todo in events.items():

            @pl.when(u == when)
            def _():
                for step in todo:
                    step()

        for p in range(pairs):
            pl.when(u == p * blocks)(functools.partial(prepare, p))
        unit(pair, key_block)
        for p in range(pairs):
            pl.when(u == p * blocks + blocks - 1)(functools.partial(close, p))

    begin(6)
    halve(4, 2)
    halve(2, 2)

    def token_term(d):
        rows = pl.ds(d * block, block)
        total = None
        for c in range(3):
            wide = jnp.concatenate([grads_ref[c * pairs + p, rows, :] for p in range(pairs)], axis=1)
            term = dot(wide, w_ref[c], NT)
            total = term if total is None else total + term
        token_ref[d] = total.astype(BF)

    token_copies = []
    for d in range(0, blocks, 2):
        token_term(d + 1)
        token_copies.append(start(push(token_ref.at[d + 1], token_sum.at[d // 2], token_core_sems, d // 2, "tensor", 1)))
    double(1, 1)
    for d in range(blocks - 2, -1, -2):
        token_term(d)
        token_copies[d // 2].wait_recv()
        token_sum[d // 2] = (token_ref[d].astype(F32) + token_sum[d // 2].astype(F32)).astype(BF)
        if d > 0:
            across = start(push(token_sum.at[d // 2], token_y.at[d // 2 - 1], token_y_sems, d // 2 - 1, "tensor", d))
    double(3, 2)
    halve(5, 0)
    double(4, 2)
    halve(6, 0)
    double(0, 1)
    double(2, 2)
    double(3, 1)
    halve(5, 1)
    double(4, 1)

    across.wait_recv()
    rows = 64
    lanes = x_ref.shape[1] // 128
    gain = gain_ref[0:1, :]

    def norm(r, carry):
        gain_term, shift_term = carry
        at = pl.ds(pl.multiple_of(r * rows, rows), rows)
        grad = token_sum[0, at, :].astype(F32)
        for h in range(blocks // 2 - 1):
            grad = grad + token_y[h, at, :].astype(F32)
        unit, scale = unit_scale(x_ref[at, :].astype(F32))
        total = rest_ref[at, :] + norm_pull(grad, unit, scale, gain)
        for c in range(lanes):
            there = pl.ds(pl.multiple_of(r * (rows * lanes), rows * lanes) + c, rows, stride=lanes)
            input_ref[there, :] = total[:, c * 128 : (c + 1) * 128]
        return (
            gain_term + jnp.sum(grad * unit, axis=0, keepdims=True),
            shift_term + jnp.sum(grad, axis=0, keepdims=True),
        )

    zero = jnp.zeros(gain.shape, F32)
    gain_term, shift_term = lax.fori_loop(0, block // rows, norm, (zero, zero))
    norm_ref[...] = early_ref[...]
    norm_ref[0:1, :] = gain_term
    norm_ref[4:5, :] = shift_term
    ts = [start(push(norm_ref, got_t.at[d - 1], t_sems, d - 1, "tensor", d)) for d in range(1, blocks)]
    halve(6, 1)
    halve(5, 2)
    for copy in ts:
        copy.wait_recv()
    sum_t[...] = tree_sum([norm_ref[...]] + [got_t[d] for d in range(blocks - 1)])
    ds = [start(push(sum_t, got_d.at[d - 1], d_sems, d - 1, "dp", d)) for d in range(1, ranks_dp)]
    double(2, 1)
    halve(6, 2)
    double(5, 2)
    double(6, 2)
    double(5, 1)
    double(6, 1)
    for copy in ds:
        copy.wait_recv()
    sums_ref[...] = tree_sum([sum_t[...]] + [got_d[d] for d in range(ranks_dp - 1)])
    for c in range(chunks):
        double(c, 0)
    for copy in [*started, *core_copies, *y_copies, *rs_copies.values(), *ag_copies.values()]:
        copy.wait_send()


def finish_stage(
    lengths, qkv, grad_heads, heads_out, logs, cosine, sine, attn, weight, tokens, rest, shared, terms, firsts, gains, early
):
    pairs3, length, _ = qkv.shape
    pairs = pairs3 // 3
    block, width = tokens.shape
    blocks = length // block
    ranks_dp = lax.axis_size("dp")
    steps = ranks_dp.bit_length() - 1
    straight = list(range(steps))
    crossed = [1, 0, *straight[2:]]
    orders = [straight, crossed, straight, crossed, straight, crossed, straight]
    assert pairs == 2 and steps >= 3
    cut = (2,) * steps
    local = shared.shape[1]
    shared = shared.reshape(blocks, *cut, local // ranks_dp, width)
    terms = [term.reshape(2, *cut, -1, term.shape[-1]) for term in terms]
    firsts = [first.reshape(*cut[1:], -1, first.shape[-1]) for first in firsts]
    wide = (*cut, width // ranks_dp, 3 * PAIR)
    shapes = [term.shape[1:] for term in terms] * 2 + [shared.shape[1:]] + [wide] * pairs
    far = (qkv, grad_heads, heads_out, cosine, sine, attn, weight, tokens, rest)
    parts = [shape[k + 1 :] for shape in shapes for k in range(steps)]
    vmem = pl.BlockSpec(memory_space=pltpu.VMEM)
    copies = pltpu.SemaphoreType.DMA
    outs = pl.pallas_call(
        functools.partial(finish_kernel, block, blocks, pairs, orders),
        out_shape=[
            jax.ShapeDtypeStruct((block * width // 128, 128), F32),
            jax.ShapeDtypeStruct((8, width), F32),
            *[jax.ShapeDtypeStruct(term.shape, BF) for term in terms],
            jax.ShapeDtypeStruct(shared.shape[1:], BF),
            jax.ShapeDtypeStruct((pairs, *wide), BF),
        ],
        in_specs=[pl.BlockSpec(memory_space=pltpu.SMEM)] + [vmem] * 8 + [pl.BlockSpec(memory_space=pl.ANY)] * 9,
        out_specs=[vmem] * 6,
        scratch_shapes=[
            *[pltpu.VMEM(array.shape, array.dtype) for array in far],
            pltpu.VMEM((8, length), jnp.int32),
            pltpu.VMEM((length, PAIR), F32),
            pltpu.VMEM((8, length), F32),
            pltpu.VMEM((pairs3, length, PAIR), BF),
            pltpu.VMEM(shared.shape[1:], BF),
            pltpu.VMEM((pairs, *wide), BF),
            pltpu.VMEM((blocks, block, width), BF),
            pltpu.VMEM((blocks // 2, *shared.shape[1:]), BF),
            pltpu.VMEM((blocks // 2 - 1, *shared.shape[1:]), BF),
            pltpu.VMEM((blocks // 2, block, width), BF),
            pltpu.VMEM((blocks // 2 - 1, block, width), BF),
            pltpu.VMEM((8, width), F32),
            pltpu.VMEM((blocks - 1, 8, width), F32),
            pltpu.VMEM((8, width), F32),
            pltpu.VMEM((ranks_dp - 1, 8, width), F32),
            *[pltpu.VMEM(shape, BF) for shape in parts],
            copies((9,)),
            copies((2, len(parts))),
            copies((2, len(parts))),
            copies((2, blocks // 2)),
            copies((2, blocks // 2 - 1)),
            copies((2, blocks // 2)),
            copies((2, blocks // 2 - 1)),
            copies((2, blocks - 1)),
            copies((2, ranks_dp - 1)),
        ],
        compiler_params=pltpu.CompilerParams(vmem_limit_bytes=62 << 20, collective_id=0, has_side_effects=True),
        name="finish_stage",
    )(lengths, *terms, *firsts, shared, logs, gains, early, *far)
    input_grad, sums, down, up, own, wides = outs
    return (
        input_grad,
        sums,
        down.reshape(width, width),
        up.reshape(2, width, -1),
        own.reshape(local, width),
        wides.reshape(pairs, width, 3 * PAIR),
    )


def body(block_in, lengths, qkv_weight, out_weight, up_weight, down_weight, norm_gain, norm_bias, cotangent):
    block, row_count, width = block_in.shape
    assert row_count == 1
    pairs = out_weight.shape[0] // PAIR
    qkv_swapped = jnp.transpose(qkv_weight, (1, 0, 2))

    qkv, attn_full, heads_mixed, logs, heads_parts, cosine, sine, rests = attend_forward(
        lengths,
        block_in.reshape(block, width),
        norm_gain,
        norm_bias,
        qkv_swapped,
        (out_weight, up_weight, down_weight),
    )
    block_out, grad_middle, grad_heads, shared, down_terms, up_terms, down_first, up_first, early = middle_stage(
        heads_parts,
        block_in.reshape(block, width),
        cotangent.reshape(block, width),
        norm_gain,
        norm_bias,
        (out_weight, up_weight, down_weight),
        rests,
    )
    input_grad, sums, down_sum, up_sums, out_sum, qkv_sums = finish_stage(
        lengths,
        qkv,
        grad_heads,
        heads_mixed,
        logs,
        cosine,
        sine,
        attn_full,
        qkv_swapped,
        block_in.reshape(block, width),
        grad_middle,
        shared,
        (down_terms, up_terms),
        (down_first, up_first),
        norm_gain,
        early,
    )
    down_grad = down_sum.astype(F32)
    up_grad = jnp.concatenate([up_sums[0], up_sums[1]], axis=1).astype(F32)
    qkv_grad = jnp.stack(
        [jnp.concatenate([qkv_sums[p, :, c * PAIR : (c + 1) * PAIR] for p in range(pairs)], axis=1) for c in range(3)]
    ).astype(F32)
    qkv_grad = jnp.transpose(qkv_grad, (1, 0, 2))
    out_grad = out_sum.astype(F32)
    gain_grad, bias_grad = sums[0:4], sums[4:8]
    return (
        block_out.reshape(block_in.shape),
        input_grad.reshape(block_in.shape),
        qkv_grad,
        out_grad,
        up_grad,
        down_grad,
        gain_grad,
        bias_grad,
    )


def solution(mesh):
    tokens, rows, columns, copied = P("tensor", "dp", None), P("tensor", None), P(None, "tensor"), P()
    heads = P(None, None, "tensor")
    return jax.shard_map(
        body,
        mesh=mesh,
        in_specs=(tokens, P("dp", None), heads, rows, columns, rows, copied, copied, tokens),
        out_specs=(tokens, tokens, heads, rows, columns, rows, copied, copied),
        check_vma=False,
    )
```

profile of v0, /device:TPU:20, one launch (start us, length us, event | category | flops | bytes accessed | tf_op | source)
XLA Modules:
  0.0 318.8 jit_solution(11728862779250051698)
XLA Ops:
  0.6 73.3 %attend_forward.1 = (bf16[2,2048,128]{2,1,0:T(8,128)(2,1)}, f32[2,8,2048]{2,1,0:T(8,128)}, bf16[8,512,128]{2,1,0:T(8,128)(2,1)}, bf16[6,2048,128]{2,1,0:T(8,128)...) custom-call(s32[1,8]{1,0:T(1,128)} %refs_0_.3, ...), custom_call_target="tpu_custom_call" | custom-call | tf_op jit(solution)/shard_map/attend_forward/pallas_call | solution.py:385
  74.0 76.9 %middle_stage.1 = (bf16[512,1024]{1,0:T(8,128)(2,1)}, f32[512,1024]{1,0:T(8,128)}, bf16[2,4,512,128]{3,2,1,0:T(8,128)(2,1)}, bf16[4,256,1024]{2,1,0:T(8,128)(2,1...) custom-call(bf16[8,512,128]{2,1,0:T(8,128)(2,1)} %get-tuple-element., ...), custom_call_target="tpu_custom_call" | custom-call | tf_op jit(solution)/shard_map/middle_stage/pallas_call | solution.py:708
  150.8 153.2 %finish_stage.1 = (f32[4096,128]{1,0:T(8,128)}, f32[8,1024]{1,0:T(8,128)}, bf16[2,2,2,2,64,1024]{5,4,3,2,1,0:T(8,128)(2,1)}, bf16[2,2,2,2,128,512]{5,4,3,2,1,0:T...) custom-call(s32[1,8]{1,0:T(1,128)} %refs_0_.3, ...), custom_call_target="tpu_custom_call" | custom-call | tf_op jit(solution)/shard_map/finish_stage/pallas_call | solution.py:1051
  304.0 0.0 copy-start.5
  304.0 1.5 slice_bitcast_fusion.5
  305.5 0.0 copy-start.4
  305.5 0.1 maximum_bitcast_fusion
  305.6 0.0 copy-done.5
  305.6 0.6 fusion.1
  306.2 0.1 maximum_bitcast_fusion.2
  306.3 0.2 copy-done.4
  306.5 1.1 bitcast_convert_fusion.1
  307.6 0.0 copy-start.2
  307.6 1.9 convert_bitcast_fusion
  309.6 0.6 copy-done.2
  310.2 0.1 fusion
  310.3 0.0 copy-start
  310.3 2.6 maximum_convert_fusion
  312.9 0.0 copy-done
  312.9 0.0 copy-start.3
  312.9 2.6 bitcast_convert_fusion
  315.5 0.0 copy-done.3
  315.5 0.0 copy-start.1
  315.5 1.0 copy.21
  316.5 1.0 copy-done.1
  317.5 1.3 copy.22
Async XLA Ops:
  304.0 1.6 copy-start.5
  305.5 1.0 copy-start.4
  307.6 2.5 copy-start.2
  310.3 2.6 copy-start
  312.9 2.6 copy-start.3
  315.5 2.0 copy-start.1
where the time goes:
time: 321 us; the launch traced here: 319 us
  Pallas kernels  303 us (94%)
  other arithmetic  8.41 us (3%)
  local copies, waits for them, and re-layouts  6.33 us (2%)
    pallas_call x1, Pallas kernels, finish_stage(): pl.pallas_call(functools.partial(finish_kernel, block, blocks, pairs, ord...  153 us
    pallas_call x1, Pallas kernels, middle_stage(): pl.pallas_call(functools.partial(middle_kernel, block, ranks, pairs), out...  76.9 us
    pallas_call x1, Pallas kernels, attend_forward(): pl.pallas_call(functools.partial(forward_kernel, block, ranks, pairs, chu...  73.3 us

commit v1 on v0

--- a/solution.py
+++ b/solution.py
@@ -443,8 +443,8 @@
 def middle_kernel(block, ranks, pairs, *refs):
     (heads_ref, x_ref, dy_ref, gains_ref, shifts_ref, *refs) = refs
     sources, refs = refs[:6], refs[6:]
-    (out_ref, rest_ref, do_ref, shared_ref, down_ref, up_ref, got_down, got_up, early_ref, *refs) = refs
-    (out_all, up_all, down_all, work_ref, mlp_ref, gmp_ref, middle_ref, proj_ref, acc_ref, gap_ref, gh_ref, *refs) = refs
+    (do_ref, down_ref, up_ref, got_down, got_up, early_ref, out_far, rest_far, shared_far, *refs) = refs
+    (out_ref, rest_ref, shared_ref, leave_sems, out_all, up_all, down_all, work_ref, mlp_ref, gmp_ref, middle_ref, proj_ref, acc_ref, gap_ref, gh_ref, *refs) = refs
     (out_sems, up_sems, down_sems, part_sems, cross_sems, mlp_sems, gmp_sems, head_sems, sum_sems) = refs
 
     mine = lax.axis_index("tensor")
@@ -631,6 +631,13 @@
         part = jnp.concatenate([heads_ref[d * pairs + p] for p in range(pairs)], axis=1)
         shared_ref[d] = dot(part, gap_ref[...], TN).astype(BF)
 
+    leaving = [
+        pltpu.make_async_copy(near_ref, far_ref, leave_sems.at[i])
+        for i, (near_ref, far_ref) in enumerate([(out_ref, out_far), (rest_ref, rest_far), (shared_ref, shared_far)])
+    ]
+    for copy in leaving:
+        copy.start()
+
     for copies in (mlp_copies, gmp_copies):
         for _, beside, _ in copies:
             beside.wait_recv()
@@ -688,6 +695,8 @@
         copy.wait_send()
     for copy in part_copies:
         copy.wait_send()
+    for copy in leaving:
+        copy.wait()
     for copies in (mlp_copies, gmp_copies):
         for group in copies:
             for copy in group:
@@ -704,23 +713,28 @@
     hbm = pl.BlockSpec(memory_space=pl.ANY)
     copies = pltpu.SemaphoreType.DMA
     assert block * 2 == width and hidden == width
+    early = [
+        jax.ShapeDtypeStruct((block, width), BF),
+        jax.ShapeDtypeStruct((block, width), F32),
+        jax.ShapeDtypeStruct((ranks, local, width), BF),
+    ]
     operands = [array for pair in zip(weights, rests) for array in pair]
-    return pl.pallas_call(
+    done = pl.pallas_call(
         functools.partial(middle_kernel, block, ranks, pairs),
         out_shape=[
-            jax.ShapeDtypeStruct((block, width), BF),
-            jax.ShapeDtypeStruct((block, width), F32),
             jax.ShapeDtypeStruct((pairs, ranks, block, PAIR), BF),
-            jax.ShapeDtypeStruct((ranks, local, width), BF),
             jax.ShapeDtypeStruct((2, 2, block // 2, width), BF),
             jax.ShapeDtypeStruct((2, 2, block, width // 2), BF),
             jax.ShapeDtypeStruct((block // 2, width), BF),
             jax.ShapeDtypeStruct((block, width // 2), BF),
             jax.ShapeDtypeStruct((8, width), F32),
+            *early,
         ],
         in_specs=[vmem] * 5 + [hbm] * 6,
-        out_specs=[vmem] * 9,
+        out_specs=[vmem] * 6 + [hbm] * 3,
         scratch_shapes=[
+            *[pltpu.VMEM(array.shape, array.dtype) for array in early],
+            copies((3,)),
             pltpu.VMEM((ranks, local, width), BF),
             pltpu.VMEM((ranks, width, hidden), BF),
             pltpu.VMEM((ranks, hidden, width), BF),
@@ -745,6 +759,8 @@
         compiler_params=pltpu.CompilerParams(vmem_limit_bytes=62 << 20, collective_id=3, has_side_effects=True),
         name="middle_stage",
     )(heads, tokens, cotangent, gains, shifts, *operands)
+    grad_heads, down, up, first_down, first_up, sums, block_out, rest, shared = done
+    return block_out, rest, grad_heads, shared, down, up, first_down, first_up, sums
 
 
 def finish_kernel(block, blocks, pairs, orders, *refs):
@@ -801,16 +817,22 @@
         at = c * steps + k
         if (c, k) in rs_copies:
             rs_copies[c, k].wait_recv()
-            term = got[at][...]
+            term = got[at]
         else:
-            term = firsts[c][...]
-        total = held(c, k)[bits[c][k]].astype(F32) + term.astype(F32)
-        got[at][...] = total.astype(BF)
-        if k + 1 < steps:
-            rs_copies[c, k + 1].start()
-        else:
-            results[c][tuple(bits[c])] = total.astype(BF)
-            ag_copies[c, k].start()
+            term = firsts[c]
+        mine_half = held(c, k).at[bits[c][k]]
+        strip = min(16, got[at].shape[-2])
+        lead = (slice(None),) * (len(got[at].shape) - 2)
+
+        @pl.loop(0, got[at].shape[-2] // strip)
+        def _(r):
+            where = (*lead, pl.ds(pl.multiple_of(r * strip, strip), strip), slice(None))
+            total = (mine_half[where].astype(F32) + term[where].astype(F32)).astype(BF)
+            got[at][where] = total
+            if k + 1 == steps:
+                results[c].at[tuple(bits[c])][where] = total
+
+        (rs_copies[c, k + 1] if k + 1 < steps else ag_copies[c, k]).start()
 
     def double(c, k):
         ag_copies[c, k].wait_recv()
@@ -1101,6 +1123,54 @@
     )
 
 
+def widen_kernel(pairs, down_ref, up_ref, own_ref, wide_ref, out_ref, input_ref, sums_ref, *refs):
+    down_out, up_out, own_out, qkv_out, out_out, input_out, gain_out, bias_out = refs
+    gain_out[...] = sums_ref[0:4, :]
+    bias_out[...] = sums_ref[4:8, :]
+    down_out[...] = down_ref[...].astype(F32)
+    half = up_ref.shape[2]
+    for side in range(2):
+        up_out[:, side * half : (side + 1) * half] = up_ref[side].astype(F32)
+    own_out[...] = own_ref[...].astype(F32)
+    for c in range(3):
+        for pair in range(pairs):
+            piece = wide_ref[pair, :, c * PAIR : (c + 1) * PAIR]
+            qkv_out[c, :, pair * PAIR : (pair + 1) * PAIR] = piece.astype(F32)
+    out_out[...] = out_ref[...]
+    input_out[...] = input_ref[...]
+
+
+def widen(down, up, own, wides, block_out, input_grad, sums):
+    pairs, width, _ = wides.shape
+    steps = 8
+    rows = lambda array: pl.BlockSpec((array.shape[0] // steps, *array.shape[1:]), lambda i: (i, 0))
+    deep = lambda array: pl.BlockSpec(
+        (array.shape[0], array.shape[1] // steps, array.shape[2]), lambda i: (0, i, 0)
+    )
+    still = lambda array: pl.BlockSpec(array.shape, lambda i: (0, 0))
+    norm = jax.ShapeDtypeStruct((sums.shape[0] // 2, width), F32)
+    qkv = jax.ShapeDtypeStruct((3, width, pairs * PAIR), F32)
+    ups = jax.ShapeDtypeStruct((up.shape[1], 2 * up.shape[2]), F32)
+    return pl.pallas_call(
+        functools.partial(widen_kernel, pairs),
+        grid=(steps,),
+        out_shape=[
+            jax.ShapeDtypeStruct(down.shape, F32),
+            ups,
+            jax.ShapeDtypeStruct(own.shape, F32),
+            qkv,
+            jax.ShapeDtypeStruct(block_out.shape, block_out.dtype),
+            jax.ShapeDtypeStruct(input_grad.shape, F32),
+            norm,
+            norm,
+        ],
+        in_specs=[rows(down), deep(up), rows(own), deep(wides), rows(block_out), rows(input_grad), still(sums)],
+        out_specs=[rows(down), rows(ups), rows(own), deep(qkv), rows(block_out), rows(input_grad), still(norm), still(norm)],
+        compiler_params=pltpu.CompilerParams(vmem_limit_bytes=62 << 20),
+        name="widen",
+    )(down, up, own, wides, block_out, input_grad, sums)
+
+
 def body(block_in, lengths, qkv_weight, out_weight, up_weight, down_weight, norm_gain, norm_bias, cotangent):
     block, row_count, width = block_in.shape
     assert row_count == 1
@@ -1142,14 +1212,10 @@
         norm_gain,
         early,
     )
-    down_grad = down_sum.astype(F32)
-    up_grad = jnp.concatenate([up_sums[0], up_sums[1]], axis=1).astype(F32)
-    qkv_grad = jnp.stack(
-        [jnp.concatenate([qkv_sums[p, :, c * PAIR : (c + 1) * PAIR] for p in range(pairs)], axis=1) for c in range(3)]
-    ).astype(F32)
+    down_grad, up_grad, out_grad, qkv_grad, block_out, input_grad, gain_grad, bias_grad = widen(
+        down_sum, up_sums, out_sum, qkv_sums, block_out, input_grad, sums
+    )
     qkv_grad = jnp.transpose(qkv_grad, (1, 0, 2))
-    out_grad = out_sum.astype(F32)
-    gain_grad, bias_grad = sums[0:4], sums[4:8]
     return (
         block_out.reshape(block_in.shape),
         input_grad.reshape(block_in.shape),

time: 321 us -> 315 us (0.981)
  Pallas kernels: 303 us -> 312 us
  other arithmetic: 8.41 us -> 0 us
  local copies, waits for them, and re-layouts: 6.33 us -> 0 us
    pallas_call x0 -> x1, Pallas kernels: none -> 10.4 us  [widen(): pl.pallas_call(functools.partial(widen_kernel, pairs), grid=(steps,), out...]
    convert_element_type x3 -> x0, other arithmetic: 6.32 us -> none  [the longest x1 2.61 us: body(): down_grad = down_sum.astype(F32)]
    unnamed x14 -> x0, local copies, waits for them, and re-layouts: 4.12 us -> none
where the time goes in v1:
time: 315 us; the launch traced here: 313 us
  Pallas kernels  312 us (99%)
    pallas_call x1, Pallas kernels, finish_stage(): pl.pallas_call(functools.partial(finish_kernel, block, blocks, pairs, ord...  153 us
    pallas_call x1, Pallas kernels, middle_stage(): pl.pallas_call(functools.partial(middle_kernel, block, ranks, pairs), out...  75.3 us
    pallas_call x1, Pallas kernels, attend_forward(): pl.pallas_call(functools.partial(forward_kernel, block, ranks, pairs, chu...  73.3 us
    pallas_call x1, Pallas kernels, widen(): pl.pallas_call(functools.partial(widen_kernel, pairs), grid=(steps,), out...  10.4 us

profile of v1, /device:TPU:20, one launch (start us, length us, event | category | flops | bytes accessed | tf_op | source)
XLA Modules:
  0.0 313.1 jit_solution(13639953268400898808)
XLA Ops:
  0.6 73.3 %attend_forward.1 = (bf16[2,2048,128]{2,1,0:T(8,128)(2,1)}, f32[2,8,2048]{2,1,0:T(8,128)}, bf16[8,512,128]{2,1,0:T(8,128)(2,1)}, bf16[6,2048,128]{2,1,0:T(8,128)...) custom-call(s32[1,8]{1,0:T(1,128)} %refs_0_.3, ...), custom_call_target="tpu_custom_call" | custom-call | tf_op jit(solution)/shard_map/attend_forward/pallas_call | solution.py:385
  74.0 75.3 %middle_stage.1 = (bf16[2,4,512,128]{3,2,1,0:T(8,128)(2,1)}, bf16[2,2,256,1024]{3,2,1,0:T(8,128)(2,1)}, bf16[2,2,512,512]{3,2,1,0:T(8,128)(2,1)}, bf16[256,1024]...) custom-call(bf16[8,512,128]{2,1,0:T(8,128)(2,1)} %get-tuple-element., ...), custom_call_target="tpu_custom_call" | custom-call | tf_op jit(solution)/shard_map/middle_stage/pallas_call | solution.py:722
  149.3 153.2 %finish_stage.1 = (f32[4096,128]{1,0:T(8,128)}, f32[8,1024]{1,0:T(8,128)}, bf16[2,2,2,2,64,1024]{5,4,3,2,1,0:T(8,128)(2,1)}, bf16[2,2,2,2,128,512]{5,4,3,2,1,0:T...) custom-call(s32[1,8]{1,0:T(1,128)} %refs_0_.3, ...), custom_call_target="tpu_custom_call" | custom-call | tf_op jit(solution)/shard_map/finish_stage/pallas_call | solution.py:1073
  302.5 10.4 %widen.1 = (f32[1024,1024]{1,0:T(8,128)}, f32[1024,1024]{1,0:T(8,128)}, f32[256,1024]{1,0:T(8,128)}, f32[3,1024,256]{2,1,0:T(8,128)}, bf16[512,1024]{1,0:T(8,128...) custom-call(bf16[1024,1024]{1,0:T(8,128)(2,1)} %bitcast.33, bf16[2,1024,512]{2,1,0:T(8,128)(2,1)} %bitcast.34, ...), custom_call_target="tpu_custom_call" | custom-call | tf_op jit(solution)/shard_map/widen/pallas_call | solution.py:1154

commit v2 on v1

--- a/solution.py
+++ b/solution.py
@@ -102,7 +102,7 @@
     weights, refs = refs[:3], refs[3:]
     mixed_ref, log_ref, heads_ref, qkv_out, attn_out, cos_out, sin_out, *refs = refs
     rests, refs = refs[:3], refs[3:]
-    scores_ref, qkv_ref, attn_ref, cos_ref, sin_ref, start_ref, out_sems, attn_sems, head_sems, own_sems, y_sems, z_sems, x_sems, core_sems = refs
+    scores_ref, qkv_ref, attn_ref, cos_ref, sin_ref, query_marks, key_marks, out_sems, attn_sems, head_sems, own_sems, y_sems, z_sems, x_sems, core_sems = refs
 
     mine = lax.axis_index("tensor")
     rank = lax.axis_index("dp")
@@ -206,13 +206,21 @@
 
     lane = lax.broadcasted_iota(jnp.int32, (64, PAIR), 1)
     sign = jnp.where(lane % HD < HD // 2, -1.0, 1.0)
+    first, past = jnp.zeros_like(lane), jnp.zeros_like(lane)
+    total = jnp.int32(0)
+    for j in range(lengths_ref.shape[1]):
+        first = jnp.where(lane % HD == j, total, first)
+        total = total + lengths_ref[0, j]
+        past = jnp.where(lane % HD == j, total, past)
 
     @pl.loop(0, ranks * block // 64)
     def _(r):
         at = pl.ds(pl.multiple_of(r * 64, 64), 64)
         spot = r * 64 + lax.broadcasted_iota(jnp.int32, (64, PAIR), 0)
         begin = document_start(lengths_ref, spot)
-        start_ref[at, :] = begin
+        inside = (spot >= first) & (spot < past)
+        query_marks[at, :] = jnp.where(inside, 1.0, 0.0).astype(BF)
+        key_marks[at, :] = jnp.where(inside, 0.0, NEG).astype(BF)
         angle = (spot - begin).astype(F32) * freq_ref[...]
         cos_ref[at, :] = jnp.cos(angle)
         sin_ref[at, :] = jnp.sin(angle) * sign
@@ -260,25 +268,27 @@
     def unit(pair, d):
         row_block = xor(d, mine, ranks)
         rows = pl.ds(pl.multiple_of(d * block, block), block)
-        begin = start_ref[pl.ds(pl.multiple_of(row_block * block, block), block), :]
         queries = qkv_ref[pair, rows, :] * HD**-0.5
+        marks = query_marks[pl.ds(pl.multiple_of(row_block * block, block), block), :]
         heads = range(PAIR // HD)
         masks = [head_mask(queries.shape, head) for head in heads]
-        parts = [jnp.where(mask, queries, jnp.zeros_like(queries)) for mask in masks]
+        parts = [jnp.where(mask, queries, marks) for mask in masks]
         column = lax.broadcasted_iota(jnp.int32, (block, 128), 1)
 
         def score(j, tops, last):
             at = pl.ds(pl.multiple_of(xor(j, mine, ranks) * block, block), block)
             keys = qkv_ref[pairs + pair, at, :]
+            marks = key_marks[pl.ds(pl.multiple_of(j * block, block), block), :]
+            keys = [jnp.where(mask, keys, marks) for mask in masks]
             tops = list(tops)
             for low in range(0, block, sub):
                 for head in heads:
-                    s = dot(parts[head], keys[low : low + sub], NT)
+                    s = dot(parts[head], keys[head][low : low + sub], NT)
                     for c in range(0, sub, 128):
-                        visible = column + (low + c) >= begin - j * block
+                        piece = s[:, c : c + 128]
                         if last:
-                            visible &= column + (low + c) <= lax.broadcasted_iota(jnp.int32, (block, 128), 0)
-                        piece = jnp.where(visible, s[:, c : c + 128], NEG)
+                            visible = column + (low + c) <= lax.broadcasted_iota(jnp.int32, (block, 128), 0)
+                            piece = jnp.where(visible, piece, NEG)
                         scores_ref[head, j, :, low + c : low + c + 128] = piece
                         tops[head] = jnp.maximum(tops[head], piece)
             return tuple(tops)
@@ -402,7 +412,8 @@
             pltpu.VMEM((ranks, block, width), BF),
             pltpu.VMEM((length, PAIR), F32),
             pltpu.VMEM((length, PAIR), F32),
-            pltpu.VMEM((length, PAIR), jnp.int32),
+            pltpu.VMEM((length, PAIR), BF),
+            pltpu.VMEM((length, PAIR), BF),
             copies((4,)),
             copies((2, 12)),
             copies((2, ranks * pairs)),
@@ -443,7 +454,7 @@
 def middle_kernel(block, ranks, pairs, *refs):
     (heads_ref, x_ref, dy_ref, gains_ref, shifts_ref, *refs) = refs
     sources, refs = refs[:6], refs[6:]
-    (do_ref, down_ref, up_ref, got_down, got_up, early_ref, out_far, rest_far, shared_far, *refs) = refs
+    (down_ref, up_ref, early_ref, do_ref, got_down, got_up, out_far, rest_far, shared_far, *refs) = refs
     (out_ref, rest_ref, shared_ref, leave_sems, out_all, up_all, down_all, work_ref, mlp_ref, gmp_ref, middle_ref, proj_ref, acc_ref, gap_ref, gh_ref, *refs) = refs
     (out_sems, up_sems, down_sems, part_sems, cross_sems, mlp_sems, gmp_sems, head_sems, sum_sems) = refs
 
@@ -621,11 +632,9 @@
         grad = dot(gap_ref[...], out_all[d], NT).astype(BF)
         for pair in range(pairs):
             piece = grad[:, pair * PAIR : (pair + 1) * PAIR]
-            if d == 0:
-                do_ref[pair, 0] = piece
-            else:
-                slot = d * pairs + pair
-                gh_ref[slot] = piece
+            slot = d * pairs + pair
+            gh_ref[slot] = piece
+            if d > 0:
                 head_copies.append(push(gh_ref.at[slot], do_ref.at[pair, d], head_sems, slot, "tensor", d))
     for d in range(ranks):
         part = jnp.concatenate([heads_ref[d * pairs + p] for p in range(pairs)], axis=1)
@@ -634,6 +643,9 @@
     leaving = [
         pltpu.make_async_copy(near_ref, far_ref, leave_sems.at[i])
         for i, (near_ref, far_ref) in enumerate([(out_ref, out_far), (rest_ref, rest_far), (shared_ref, shared_far)])
+    ]
+    leaving += [
+        pltpu.make_async_copy(gh_ref.at[pair], do_ref.at[pair, 0], leave_sems.at[3 + pair]) for pair in range(pairs)
     ]
     for copy in leaving:
         copy.start()
@@ -722,19 +734,19 @@
     done = pl.pallas_call(
         functools.partial(middle_kernel, block, ranks, pairs),
         out_shape=[
-            jax.ShapeDtypeStruct((pairs, ranks, block, PAIR), BF),
             jax.ShapeDtypeStruct((2, 2, block // 2, width), BF),
             jax.ShapeDtypeStruct((2, 2, block, width // 2), BF),
+            jax.ShapeDtypeStruct((8, width), F32),
+            jax.ShapeDtypeStruct((pairs, ranks, block, PAIR), BF),
             jax.ShapeDtypeStruct((block // 2, width), BF),
             jax.ShapeDtypeStruct((block, width // 2), BF),
-            jax.ShapeDtypeStruct((8, width), F32),
             *early,
         ],
         in_specs=[vmem] * 5 + [hbm] * 6,
-        out_specs=[vmem] * 6 + [hbm] * 3,
+        out_specs=[vmem] * 3 + [hbm] * 6,
         scratch_shapes=[
             *[pltpu.VMEM(array.shape, array.dtype) for array in early],
-            copies((3,)),
+            copies((3 + pairs,)),
             pltpu.VMEM((ranks, local, width), BF),
             pltpu.VMEM((ranks, width, hidden), BF),
             pltpu.VMEM((ranks, hidden, width), BF),
@@ -759,16 +771,17 @@
         compiler_params=pltpu.CompilerParams(vmem_limit_bytes=62 << 20, collective_id=3, has_side_effects=True),
         name="middle_stage",
     )(heads, tokens, cotangent, gains, shifts, *operands)
-    grad_heads, down, up, first_down, first_up, sums, block_out, rest, shared = done
+    down, up, sums, grad_heads, first_down, first_up, block_out, rest, shared = done
     return block_out, rest, grad_heads, shared, down, up, first_down, first_up, sums
 
 
 def finish_kernel(block, blocks, pairs, orders, *refs):
-    (lengths_ref, down_ref, up_ref, first_down, first_up, shared_ref, log_ref, gain_ref, early_ref, *refs) = refs
-    far_refs, refs = refs[:9], refs[9:]
+    (lengths_ref, first_down, first_up, log_ref, gain_ref, early_ref, *refs) = refs
+    far_refs, refs = refs[:12], refs[12:]
     (input_ref, sums_ref, down_out, up_out, own_out, qkv_out, *refs) = refs
-    near_refs, refs = refs[:9], refs[9:]
-    (qkv_ref, do_ref, o_ref, cos_ref, sin_ref, attn_ref, w_ref, x_ref, rest_ref) = near_refs
+    near_refs, refs = refs[:12], refs[12:]
+    (down_ref, up_ref, shared_ref, qkv_ref, do_ref, o_ref, cos_ref, sin_ref, attn_ref, w_ref, x_ref, rest_ref) = near_refs
+    down_far, up_far, shared_far = far_refs[:3]
     (start_ref, dq_ref, inner_ref, grads_ref, own_ref, wide_ref, token_ref, core_sum, got_y, *refs) = refs
     (token_sum, token_y, norm_ref, got_t, sum_t, got_d, *refs) = refs
     chunks, steps = len(orders), len(orders[0])
@@ -805,7 +818,8 @@
         for k in range(steps):
             far = 1 << orders[c][k]
             if k > 0 or c not in firsts:
-                source = held(c, k).at[1 - bits[c][k]]
+                source = {2: down_far.at[1], 3: up_far.at[1]}.get(c, held(c, k)) if k == 0 else held(c, k)
+                source = source.at[1 - bits[c][k]]
                 rs_copies[c, k] = push(source, got[c * steps + k], rs_sems, c * steps + k, "dp", far)
             region = results[c].at[tuple(bits[c][: k + 1])]
             ag_copies[c, k] = push(region, region, ag_sems, c * steps + k, "dp", far)
@@ -840,7 +854,7 @@
             ag_copies[c, k - 1].start()
 
     core_copies = [
-        push(shared_ref.at[d + 1], core_sum.at[d // 2], core_sems, d // 2, "tensor", 1) for d in range(0, blocks, 2)
+        push(shared_far.at[d + 1], core_sum.at[d // 2], core_sems, d // 2, "tensor", 1) for d in range(0, blocks, 2)
     ]
     y_copies = [
         push(core_sum.at[h], got_y.at[h - 1], y_sems, h - 1, "tensor", 2 * h) for h in range(1, blocks // 2)
@@ -929,10 +943,12 @@
         copy.start()
     begin(3)
     begin(2)
+    for load in loads[:3]:
+        load.wait()
     halve(0, 0)
     halve(1, 0)
     start_ref[...] = document_start(lengths_ref, lax.broadcasted_iota(jnp.int32, start_ref.shape, 1))
-    for load in loads[:5]:
+    for load in loads[3:8]:
         load.wait()
     slots = pairs * blocks
     halving = lambda *steps: [functools.partial(halve, c, k) for c, k in steps]
@@ -941,7 +957,7 @@
     events = {
         0: [pair_up],
         2: [settle] + beginning(4) + halving((0, 1), (3, 0), (1, 1), (2, 0)),
-        3: [lambda: [load.wait() for load in loads[5:]]],
+        3: [lambda: [load.wait() for load in loads[8:]]],
         4: beginning(5) + halving((0, 2), (4, 0), (3, 1), (1, 2)),
         5: halving((2, 1)),
         6: halving((4, 1)) + doubling((0, 2)),
@@ -1066,7 +1082,7 @@
     firsts = [first.reshape(*cut[1:], -1, first.shape[-1]) for first in firsts]
     wide = (*cut, width // ranks_dp, 3 * PAIR)
     shapes = [term.shape[1:] for term in terms] * 2 + [shared.shape[1:]] + [wide] * pairs
-    far = (qkv, grad_heads, heads_out, cosine, sine, attn, weight, tokens, rest)
+    far = (*terms, shared, qkv, grad_heads, heads_out, cosine, sine, attn, weight, tokens, rest)
     parts = [shape[k + 1 :] for shape in shapes for k in range(steps)]
     vmem = pl.BlockSpec(memory_space=pltpu.VMEM)
     copies = pltpu.SemaphoreType.DMA
@@ -1079,7 +1095,7 @@
             jax.ShapeDtypeStruct(shared.shape[1:], BF),
             jax.ShapeDtypeStruct((pairs, *wide), BF),
         ],
-        in_specs=[pl.BlockSpec(memory_space=pltpu.SMEM)] + [vmem] * 8 + [pl.BlockSpec(memory_space=pl.ANY)] * 9,
+        in_specs=[pl.BlockSpec(memory_space=pltpu.SMEM)] + [vmem] * 5 + [pl.BlockSpec(memory_space=pl.ANY)] * 12,
         out_specs=[vmem] * 6,
         scratch_shapes=[
             *[pltpu.VMEM(array.shape, array.dtype) for array in far],
@@ -1099,7 +1115,7 @@
             pltpu.VMEM((8, width), F32),
             pltpu.VMEM((ranks_dp - 1, 8, width), F32),
             *[pltpu.VMEM(shape, BF) for shape in parts],
-            copies((9,)),
+            copies((12,)),
             copies((2, len(parts))),
             copies((2, len(parts))),
             copies((2, blocks // 2)),
@@ -1111,7 +1127,7 @@
         ],
         compiler_params=pltpu.CompilerParams(vmem_limit_bytes=62 << 20, collective_id=0, has_side_effects=True),
         name="finish_stage",
-    )(lengths, *terms, *firsts, shared, logs, gains, early, *far)
+    )(lengths, *firsts, logs, gains, early, *far)
     input_grad, sums, down, up, own, wides = outs
     return (
         input_grad,

time: 315 us -> 313 us (level)
  no operation moved by 1% of the time
where the time goes in v2:
time: 313 us; the launch traced here: 311 us
  Pallas kernels  310 us (99%)
    pallas_call x1, Pallas kernels, finish_stage(): pl.pallas_call(functools.partial(finish_kernel, block, blocks, pairs, ord...  151 us
    pallas_call x1, Pallas kernels, middle_stage(): pl.pallas_call(functools.partial(middle_kernel, block, ranks, pairs), out...  74.8 us
    pallas_call x1, Pallas kernels, attend_forward(): pl.pallas_call(functools.partial(forward_kernel, block, ranks, pairs, chu...  73.4 us
    pallas_call x1, Pallas kernels, widen(): pl.pallas_call(functools.partial(widen_kernel, pairs), grid=(steps,), out...  10.4 us

profile of v2, /device:TPU:20, one launch (start us, length us, event | category | flops | bytes accessed | tf_op | source)
XLA Modules:
  0.0 310.9 jit_solution(5685942618917972761)
XLA Ops:
  0.6 73.4 %attend_forward.1 = (bf16[2,2048,128]{2,1,0:T(8,128)(2,1)}, f32[2,8,2048]{2,1,0:T(8,128)}, bf16[8,512,128]{2,1,0:T(8,128)(2,1)}, bf16[6,2048,128]{2,1,0:T(8,128)...) custom-call(s32[1,8]{1,0:T(1,128)} %refs_0_.3, ...), custom_call_target="tpu_custom_call" | custom-call | tf_op jit(solution)/shard_map/attend_forward/pallas_call | solution.py:395
  74.0 74.8 %middle_stage.1 = (bf16[2,2,256,1024]{3,2,1,0:T(8,128)(2,1)}, bf16[2,2,512,512]{3,2,1,0:T(8,128)(2,1)}, f32[8,1024]{1,0:T(8,128)}, bf16[2,4,512,128]{3,2,1,0:T(8...) custom-call(bf16[8,512,128]{2,1,0:T(8,128)(2,1)} %get-tuple-element., ...), custom_call_target="tpu_custom_call" | custom-call | tf_op jit(solution)/shard_map/middle_stage/pallas_call | solution.py:734
  148.8 151.5 %finish_stage.1 = (f32[4096,128]{1,0:T(8,128)}, f32[8,1024]{1,0:T(8,128)}, bf16[2,2,2,2,64,1024]{5,4,3,2,1,0:T(8,128)(2,1)}, bf16[2,2,2,2,128,512]{5,4,3,2,1,0:T...) custom-call(s32[1,8]{1,0:T(1,128)} %refs_0_.3, ...), custom_call_target="tpu_custom_call" | custom-call | tf_op jit(solution)/shard_map/finish_stage/pallas_call | solution.py:1089
  300.3 10.4 %widen.1 = (f32[1024,1024]{1,0:T(8,128)}, f32[1024,1024]{1,0:T(8,128)}, f32[256,1024]{1,0:T(8,128)}, f32[3,1024,256]{2,1,0:T(8,128)}, bf16[512,1024]{1,0:T(8,128...) custom-call(bf16[1024,1024]{1,0:T(8,128)(2,1)} %bitcast.33, bf16[2,1024,512]{2,1,0:T(8,128)(2,1)} %bitcast.34, ...), custom_call_target="tpu_custom_call" | custom-call | tf_op jit(solution)/shard_map/widen/pallas_call | solution.py:1170

commit v3 on v2

--- a/solution.py
+++ b/solution.py
@@ -335,15 +335,16 @@
     units = pairs * ranks
     events = {
         0: [lambda: to_x(2), lambda: to_z(3), lambda: to_z(4), lambda: to_core(0), lambda: to_core(1)],
-        3: [lambda: to_x(3)],
-        5: [lambda: to_core(2)],
     }
+    far = lax.div(mine, 2)
 
     @pl.loop(0, units)
     def _(u):
         pair, d = lax.rem(u, pairs), ranks - 1 - lax.div(u, pairs)
         unit(pair, d)
         pl.when(d > 0)(lambda: head_copy(pair, d).start())
+        pl.when(u == 2 + 3 * far)(lambda: to_x(3))
+        pl.when(u == 5 + far)(lambda: to_core(2))
         for when, steps in events.items():
 
             @pl.when(u == min(when, units - 1))
@@ -1158,7 +1159,7 @@
 
 def widen(down, up, own, wides, block_out, input_grad, sums):
     pairs, width, _ = wides.shape
-    steps = 8
+    steps = 4
     rows = lambda array: pl.BlockSpec((array.shape[0] // steps, *array.shape[1:]), lambda i: (i, 0))
     deep = lambda array: pl.BlockSpec(
         (array.shape[0], array.shape[1] // steps, array.shape[2]), lambda i: (0, i, 0)

time: 313 us -> 310 us (level)
  no operation moved by 1% of the time
where the time goes in v3:
time: 310 us; the launch traced here: 309 us
  Pallas kernels  308 us (99%)
    pallas_call x1, Pallas kernels, finish_stage(): pl.pallas_call(functools.partial(finish_kernel, block, blocks, pairs, ord...  149 us
    pallas_call x1, Pallas kernels, middle_stage(): pl.pallas_call(functools.partial(middle_kernel, block, ranks, pairs), out...  77.7 us
    pallas_call x1, Pallas kernels, attend_forward(): pl.pallas_call(functools.partial(forward_kernel, block, ranks, pairs, chu...  71.2 us
    pallas_call x1, Pallas kernels, widen(): pl.pallas_call(functools.partial(widen_kernel, pairs), grid=(steps,), out...  9.81 us

profile of v3, /device:TPU:20, one launch (start us, length us, event | category | flops | bytes accessed | tf_op | source)
XLA Modules:
  0.0 308.7 jit_solution(6694906621048256537)
XLA Ops:
  0.6 71.2 %attend_forward.1 = (bf16[2,2048,128]{2,1,0:T(8,128)(2,1)}, f32[2,8,2048]{2,1,0:T(8,128)}, bf16[8,512,128]{2,1,0:T(8,128)(2,1)}, bf16[6,2048,128]{2,1,0:T(8,128)...) custom-call(s32[1,8]{1,0:T(1,128)} %refs_0_.3, ...), custom_call_target="tpu_custom_call" | custom-call | tf_op jit(solution)/shard_map/attend_forward/pallas_call | solution.py:396
  71.8 77.7 %middle_stage.1 = (bf16[2,2,256,1024]{3,2,1,0:T(8,128)(2,1)}, bf16[2,2,512,512]{3,2,1,0:T(8,128)(2,1)}, f32[8,1024]{1,0:T(8,128)}, bf16[2,4,512,128]{3,2,1,0:T(8...) custom-call(bf16[8,512,128]{2,1,0:T(8,128)(2,1)} %get-tuple-element., ...), custom_call_target="tpu_custom_call" | custom-call | tf_op jit(solution)/shard_map/middle_stage/pallas_call | solution.py:735
  149.5 149.2 %finish_stage.1 = (f32[4096,128]{1,0:T(8,128)}, f32[8,1024]{1,0:T(8,128)}, bf16[2,2,2,2,64,1024]{5,4,3,2,1,0:T(8,128)(2,1)}, bf16[2,2,2,2,128,512]{5,4,3,2,1,0:T...) custom-call(s32[1,8]{1,0:T(1,128)} %refs_0_.3, ...), custom_call_target="tpu_custom_call" | custom-call | tf_op jit(solution)/shard_map/finish_stage/pallas_call | solution.py:1090
  298.7 9.8 %widen.1 = (f32[1024,1024]{1,0:T(8,128)}, f32[1024,1024]{1,0:T(8,128)}, f32[256,1024]{1,0:T(8,128)}, f32[3,1024,256]{2,1,0:T(8,128)}, bf16[512,1024]{1,0:T(8,128...) custom-call(bf16[1024,1024]{1,0:T(8,128)(2,1)} %bitcast.33, bf16[2,1024,512]{2,1,0:T(8,128)(2,1)} %bitcast.34, ...), custom_call_target="tpu_custom_call" | custom-call | tf_op jit(solution)/shard_map/widen/pallas_call | solution.py:1171

commit v4 on v3

--- a/solution.py
+++ b/solution.py
@@ -334,7 +334,8 @@
         copy.start()
     units = pairs * ranks
     events = {
-        0: [lambda: to_x(2), lambda: to_z(3), lambda: to_z(4), lambda: to_core(0), lambda: to_core(1)],
+        0: [lambda: to_x(2), lambda: to_z(3), lambda: to_z(4), lambda: to_core(0)],
+        1: [lambda: to_core(1)],
     }
     far = lax.div(mine, 2)
 

time: 310 us -> 310 us (level)
  no operation moved by 1% of the time
where the time goes in v4:
time: 310 us; the launch traced here: 309 us
  Pallas kernels  308 us (99%)
    pallas_call x1, Pallas kernels, finish_stage(): pl.pallas_call(functools.partial(finish_kernel, block, blocks, pairs, ord...  149 us
    pallas_call x1, Pallas kernels, middle_stage(): pl.pallas_call(functools.partial(middle_kernel, block, ranks, pairs), out...  77.7 us
    pallas_call x1, Pallas kernels, attend_forward(): pl.pallas_call(functools.partial(forward_kernel, block, ranks, pairs, chu...  71.2 us
    pallas_call x1, Pallas kernels, widen(): pl.pallas_call(functools.partial(widen_kernel, pairs), grid=(steps,), out...  9.81 us

profile of v4, /device:TPU:20, one launch (start us, length us, event | category | flops | bytes accessed | tf_op | source)
XLA Modules:
  0.0 308.7 jit_solution(1116603705566447628)
XLA Ops:
  0.6 71.2 %attend_forward.1 = (bf16[2,2048,128]{2,1,0:T(8,128)(2,1)}, f32[2,8,2048]{2,1,0:T(8,128)}, bf16[8,512,128]{2,1,0:T(8,128)(2,1)}, bf16[6,2048,128]{2,1,0:T(8,128)...) custom-call(s32[1,8]{1,0:T(1,128)} %refs_0_.3, ...), custom_call_target="tpu_custom_call" | custom-call | tf_op jit(solution)/shard_map/attend_forward/pallas_call | solution.py:397
  71.8 77.7 %middle_stage.1 = (bf16[2,2,256,1024]{3,2,1,0:T(8,128)(2,1)}, bf16[2,2,512,512]{3,2,1,0:T(8,128)(2,1)}, f32[8,1024]{1,0:T(8,128)}, bf16[2,4,512,128]{3,2,1,0:T(8...) custom-call(bf16[8,512,128]{2,1,0:T(8,128)(2,1)} %get-tuple-element., ...), custom_call_target="tpu_custom_call" | custom-call | tf_op jit(solution)/shard_map/middle_stage/pallas_call | solution.py:736
  149.5 149.2 %finish_stage.1 = (f32[4096,128]{1,0:T(8,128)}, f32[8,1024]{1,0:T(8,128)}, bf16[2,2,2,2,64,1024]{5,4,3,2,1,0:T(8,128)(2,1)}, bf16[2,2,2,2,128,512]{5,4,3,2,1,0:T...) custom-call(s32[1,8]{1,0:T(1,128)} %refs_0_.3, ...), custom_call_target="tpu_custom_call" | custom-call | tf_op jit(solution)/shard_map/finish_stage/pallas_call | solution.py:1091
  298.8 9.8 %widen.1 = (f32[1024,1024]{1,0:T(8,128)}, f32[1024,1024]{1,0:T(8,128)}, f32[256,1024]{1,0:T(8,128)}, f32[3,1024,256]{2,1,0:T(8,128)}, bf16[512,1024]{1,0:T(8,128...) custom-call(bf16[1024,1024]{1,0:T(8,128)(2,1)} %bitcast.33, bf16[2,1024,512]{2,1,0:T(8,128)(2,1)} %bitcast.34, ...), custom_call_target="tpu_custom_call" | custom-call | tf_op jit(solution)/shard_map/widen/pallas_call | solution.py:1172
